TPU v7x, 256 devices: a whole 4x4x8 slice. The times are simulated.
256 devices in a mesh: tm: 32 (over y, z), eval: 8 (over x, core).
Axes of the slice: x: 4, y: 4, z: 8, core: 2. Of those that a mesh axis runs over, the one named last changes fastest.
Arguments:
- hidden: bfloat16 [512, 1024, 1536], P('tm', 'eval'), may hold values from -9 to 9
- modulation: float32 [512, 2, 1536], P('tm'), may hold values from -2 to 3
- head_weight: bfloat16 [64, 1536], replicated, may hold values from -1 to 1
- real_score: bfloat16 [64, 21, 16, 4096], P('eval', None, None, 'tm'), may hold values from -152917 to 152917
- fake_score: bfloat16 [64, 21, 16, 4096], P('eval', None, None, 'tm'), may hold values from -152917 to 152917
- window_start: int32 [64], P('eval'), may hold values from 0 to 491, as said below
- timestep: int32 [64], P('eval'), may hold values from 20 to 999
Outputs:
- d_hidden: bfloat16 [512, 1024, 1536], P('tm', 'eval')
- head_grad: float32 [64, 1536], replicated
- mod_grad: float32 [512, 2, 1536], P('tm')
Inputs may be any that keep to these rules, and one draw needn't show every extreme that they name: `window_start`: every window lies inside the rollout; one window starts at frame 0 and one at the last possible frame.
All inputs are finite; a program needn't handle non-finite values.
Results may differ from a plain program's by a relative error of at most 0.0012.
The roundings to bfloat16 on the way count: a program that leaves them out, or rounds other values in their place, can miss the bound.
Values may be sent and summed in bfloat16 or wider, within the bound.
No kernel may reach another device: no remote copies, remote signals or barrier semaphores. Data moves between devices by JAX's collectives and lax.ppermute only.
A program may use at most 128 MiB of HBM per device.

v0:
```python
import jax
import jax.numpy as jnp
from jax import lax
from jax.sharding import PartitionSpec as P

C = 16
PATCH = 4
WIN = 21
TOK = 1024


def layer_norm(values_in):
    values = values_in.astype(jnp.float32)
    center = jnp.mean(values, axis=-1, keepdims=True)
    shifted = values - center
    inv_std = lax.rsqrt(jnp.mean(shifted * shifted, axis=-1, keepdims=True) + 1e-06)
    return (shifted * inv_std, inv_std)


def per_device(hidden, modulation, head_weight, real_score, fake_score, window_start, timestep):
    frames_dev, tok_dev, width = hidden.shape
    shift = modulation[:, 0][:, None, :]
    scale = modulation[:, 1][:, None, :]
    normed, inv_std = layer_norm(hidden)
    adapted = (normed * (1.0 + scale) + shift).astype(jnp.bfloat16)
    head_out = jnp.einsum("ftd,od->fto", adapted, head_weight, preferred_element_type=jnp.float32)
    latent = head_out.astype(jnp.bfloat16).reshape(frames_dev, tok_dev, C, PATCH)
    latent = latent.transpose(0, 2, 1, 3).reshape(frames_dev, C, tok_dev * PATCH)
    frame_whole = lax.all_gather(latent, "eval", axis=2, tiled=True)
    latent_all = lax.all_to_all(frame_whole, "tm", split_axis=2, concat_axis=0, tiled=True)
    pixel_block = latent_all.shape[2]
    frame_index = window_start[:, None] + jnp.arange(WIN, dtype=jnp.int32)[None, :]
    window_latent = latent_all[frame_index].astype(jnp.float32)
    real_values = real_score.astype(jnp.float32)
    fake_values = fake_score.astype(jnp.float32)
    abs_sums = jnp.sum(jnp.abs(window_latent - real_values), axis=(1, 2, 3))
    totals = lax.psum(abs_sums, "tm")
    normalizer = totals / (WIN * C * PATCH * TOK) + 1e-05
    weight = timestep.astype(jnp.float32) / 1000.0 / normalizer
    window_grad = weight[:, None, None, None] * (fake_values - real_values)
    group_grad = (
        jnp.zeros(latent_all.shape, jnp.float32)
        .at[frame_index.reshape(-1)]
        .add(window_grad.reshape(-1, C, pixel_block))
    )
    home = lax.all_to_all(group_grad, "tm", split_axis=0, concat_axis=2, tiled=True)
    owner_grad = lax.psum_scatter(home, "eval", scatter_dimension=2, tiled=True)
    upstream = owner_grad.reshape(frames_dev, C, tok_dev, PATCH).transpose(0, 2, 1, 3)
    upstream = upstream.reshape(frames_dev, tok_dev, C * PATCH).astype(jnp.bfloat16)
    d_adapted = jnp.einsum("fto,od->ftd", upstream, head_weight, preferred_element_type=jnp.float32)
    head_part = jnp.einsum("fto,ftd->od", upstream, adapted, preferred_element_type=jnp.float32)
    mod_part = jnp.stack([jnp.sum(d_adapted, axis=1), jnp.sum(d_adapted * normed, axis=1)], axis=1)
    head_grad = lax.psum(head_part, ("tm", "eval"))
    mod_grad = lax.psum(mod_part, "eval")
    d_normed = d_adapted * (1.0 + scale)
    d_hidden = inv_std * (
        d_normed
        - jnp.mean(d_normed, axis=-1, keepdims=True)
        - normed * jnp.mean(d_normed * normed, axis=-1, keepdims=True)
    )
    return (d_hidden.astype(jnp.bfloat16), head_grad, mod_grad)


def solution(mesh):
    placed = (
        P("tm", "eval", None),
        P("tm", None, None),
        P(),
        P("eval", None, None, "tm"),
        P("eval", None, None, "tm"),
        P("eval"),
        P("eval"),
    )
    return jax.shard_map(
        per_device,
        mesh=mesh,
        in_specs=placed,
        out_specs=(P("tm", "eval", None), P(), P("tm", None, None)),
        check_vma=False,
    )
```

profile of v0, /device:TPU:1, one launch (start us, length us, event | category | flops | bytes accessed | tf_op | source)
XLA Modules:
  0.0 757.5 jit_solution(7772980234880290092)
XLA Ops:
  7.2 3.8 convert_reduce_fusion
  11.1 4.6 fusion.13
  15.9 3.1 fusion.24
  19.0 3.2 copy.49
  22.2 2.3 copy.50
  24.5 32.2 %all-gather.2.cloned.1.call-done = bf16[16,16,4096]{2,1,0:T(8,128)(2,1)} async-done(((bf16[16,16,512]{2,1,0:T(8,128)(2,1)}), bf16[16,16,4096]{2,1,0:T(8,128)(2,1)}) %all-gather.2.cloned.1.call-update) | async-done | bytes 2097168 | tf_op jit(solution)/shard_map/all_gather | solution.py:29
  56.7 15.4 %copy.51 = bf16[16,16,4096]{1,0,2:T(8,128)(2,1)} copy(bf16[16,16,4096]{2,1,0:T(8,128)(2,1)} %all-gather.2.cloned.1.call-done) | data formatting | bytes 4194304 | tf_op jit(solution)/shard_map/all_gather | solution.py:29
  72.0 20.8 %reshape.132 = bf16[32,2,16384]{2,1,0:T(2,128)(2,1)} reshape(bf16[4096,16,16]{2,1,0:T(8,128)(2,1)} %bitcast.43) | data formatting | bytes 4194304
  92.8 9.6 %all-to-all-start = ((bf16[32,2,16384]{2,1,0:T(2,128)(2,1)}), bf16[32,2,16384]{2,1,0:T(2,128)(2,1)S(1)}, u32[]{:S(2)}, u32[]{:S(2)}) async-start(bf16[32,2,16384]{2,1,0:T(2,128)(2,1)} %reshape.132), calls=%async_computation | async-start | bytes 4194304 | tf_op jit(solution)/shard_map/all_to_all | solution.py:30
  102.8 48.5 %all-to-all-done = bf16[32,2,16384]{2,1,0:T(2,128)(2,1)S(1)} async-done(((bf16[32,2,16384]{2,1,0:T(2,128)(2,1)}), bf16[32,2,16384]{2,1,0:T(2,128)(2,1)S(1)}, u32[]{:S(2)}, u32[]{:S(2)}) %all-to-all-start) | async-done | bytes 2097184 | tf_op jit(solution)/shard_map/all_to_all | solution.py:30
  151.3 14.4 %reshape.133 = bf16[4096,16,16]{2,1,0:T(8,128)(2,1)} reshape(bf16[32,2,16384]{2,1,0:T(2,128)(2,1)S(1)} %all-to-all-done) | data formatting | bytes 4194304
  165.7 14.4 %copy.53 = bf16[32,16,16,128]{3,2,1,0:T(8,128)(2,1)S(1)} copy(bf16[32,16,16,128]{2,1,3,0:T(8,128)(2,1)} %bitcast.44) | data formatting | bytes 4194304 | tf_op jit(solution)/shard_map/all_to_all | solution.py:30
  183.1 60.2 %psum.21 = f32[8]{0:T(128)S(1)} all-reduce(f32[8]{0:T(128)S(1)} %fusion.22), channel_id=1, replica_groups=mesh['tm'=32,'eval'=8] {'tm'}, use_global_device_ids=true, to_apply=%region_3.0 | all-reduce | flops 8 | bytes 64 | tf_op jit(solution)/shard_map/psum | solution.py:37
  247.0 19.7 %scatter_fusion = f32[512,16,128]{2,1,0:T(8,128)} fusion(f32[512,16,128]{2,1,0:T(8,128)} %broadcast_in_dim.2, s32[168]{0:T(256)S(1)} %bitcast.59, f32[168,16,128]{2,1,0:T(8,128)S(1)} %bitcast.51), kind=kCustom, calls=%fused_computation.1 | custom fusion | flops 344064 | bytes 4129440 | tf_op jit(solution)/shard_map/scatter-add | solution.py:44
  266.7 83.4 %all_to_all.36 = f32[512,16,128]{2,1,0:T(8,128)S(1)} all-to-all(f32[512,16,128]{2,1,0:T(8,128)} %scatter_fusion), channel_id=1, replica_groups=mesh['tm'=32,'eval'=8] {'tm'}, dimensions={0} | all-to-all | bytes 8388608 | tf_op jit(solution)/shard_map/all_to_all | solution.py:46
  350.1 2.5 copy.76
  352.7 50.7 %reduce-scatter.2.cloned.1.call-done = f32[16,16,512]{2,1,0:T(8,128)} async-done(((f32[16,16,4096]{2,1,0:T(8,128)}), f32[16,16,512]{2,1,0:T(8,128)}) %reduce-scatter.2.cloned.1.call-update) | async-done | bytes 524304 | tf_op jit(solution)/shard_map/reduce_scatter | solution.py:47
  404.5 2.8 copy.55
  407.3 4.0 copy.56
  411.3 10.1 %fusion.12 = (f32[16,1536]{1,0:T(8,128)S(1)}, f32[16,128]{1,0:T(8,128)S(1)}, f32[16,128]{1,0:T(8,128)S(1)}, f32[16,1536]{1,0:T(8,128)S(1)}, f32[16,128,1536]{2,1,0:T(8,128)}) fusion(bf16[16,128,1536]{2,1,0:T(8,128)(2,1)} %param.7, f32[16,128]{1,0:T(8,128)S(1)} %add_rsqrt_fusion, f32[16,128]{1,0:T(8,128)S(1)} %broadcast_multiply_fusion.2, ...), kind=kOutput, calls=%fused_computation.16 | convolution fusion | flops 434057216 | bytes 19660800 | tf_op jit(solution)/shard_map/fto,od->ftd/dot_general | solution.py:50
  421.4 3.5 fusion.18
  426.2 10.5 %fusion.11 = bf16[16,128,1536]{2,1,0:T(8,128)(2,1)} fusion(bf16[16,128,1536]{2,1,0:T(8,128)(2,1)} %param.7, f32[16,128,1536]{2,1,0:T(8,128)} %get-tuple-element.24, f32[16,128]{1,0:T(8,128)S(1)} %broadcast_multiply_fusion, f32[16,128]{1,0:T(8,128)S(1)} %broadcast_multiply_fusion.1, f32[16,1536]{1,0:T(8,128)S(1)} %get-tuple-element.26, ...), kind=kLoop, calls=%fused_computation.15 | loop fusion | flops 28311552 | bytes 25296896 | tf_op jit(solution)/shard_map/convert_element_type | solution.py:61
  436.7 53.9 %all-reduce.5.cloned.1.call-done = f32[16,2,1536]{2,0,1:T(8,128)} async-done(((f32[16,2,1536]{2,0,1:T(8,128)}), f32[16,2,1536]{2,0,1:T(8,128)}) %all-reduce.5.cloned.1.call-update) | async-done | bytes 196624 | tf_op jit(solution)/shard_map/psum | solution.py:54
  492.3 256.9 %all-reduce.3.cloned.1.call-done = f32[64,1536]{1,0:T(8,128)} async-done(((f32[64,1536]{1,0:T(8,128)}), f32[64,1536]{1,0:T(8,128)}) %all-reduce.3.cloned.1.call-update) | async-done | bytes 393232 | tf_op jit(solution)/shard_map/psum | solution.py:53
  (46 shorter events, 13.2 us)
Async XLA Ops:
  7.2 8.7 %copy-start = (bf16[64,1536]{1,0:T(8,128)(2,1)S(1)}, bf16[64,1536]{1,0:T(8,128)(2,1)}, u32[]{:S(2)}) copy-start(bf16[64,1536]{1,0:T(8,128)(2,1)} %param.9) | copy-start | bytes 589828
  7.2 8.5 %copy-start.3 = (f32[16,2,1536]{2,1,0:T(2,128)S(1)}, f32[16,2,1536]{2,1,0:T(2,128)}, u32[]{:S(2)}) copy-start(f32[16,2,1536]{2,1,0:T(2,128)} %param.8) | copy-start | bytes 589828
  7.2 49.5 %all-gather.2.cloned.1.call-start = ((), (), s32[]{:S(2)}) async-start(), calls=%async_computation.3 | async-start | bytes 2359296 | tf_op jit(solution)/shard_map/all_gather | solution.py:29
  7.2 8.7 %copy-start.1 = (bf16[16,128,1536]{2,1,0:T(8,128)(2,1)S(1)}, bf16[16,128,1536]{2,1,0:T(8,128)(2,1)}, u32[]{:S(2)}) copy-start(bf16[16,128,1536]{2,1,0:T(8,128)(2,1)} %param.7) | copy-start | bytes 18874372
  72.0 30.4 %copy-start.4 = (s32[8]{0:T(128)S(1)}, s32[8]{0:T(128)}, u32[]{:S(2)}) copy-start(s32[8]{0:T(128)} %param.12) | copy-start | bytes 100
  92.8 58.5 %all-to-all-start = ((bf16[32,2,16384]{2,1,0:T(2,128)(2,1)}), bf16[32,2,16384]{2,1,0:T(2,128)(2,1)S(1)}, u32[]{:S(2)}, u32[]{:S(2)}) async-start(bf16[32,2,16384]{2,1,0:T(2,128)(2,1)} %reshape.132), calls=%async_computation | async-start | bytes 4194304 | tf_op jit(solution)/shard_map/all_to_all | solution.py:30
  102.4 301.0 %reduce-scatter.2.cloned.1.call-start = ((), (), s32[]{:S(2)}) async-start(), calls=%async_computation.4 | async-start | bytes 4718592 | tf_op jit(solution)/shard_map/reduce_scatter | solution.py:47
  165.7 16.0 %copy-start.2 = (bf16[8,21,16,128]{3,2,1,0:T(8,128)(2,1)S(1)}, bf16[8,21,16,128]{3,2,1,0:T(8,128)(2,1)}, u32[]{:S(2)}) copy-start(bf16[8,21,16,128]{3,2,1,0:T(8,128)(2,1)} %param.10) | copy-start | bytes 2064388
  165.7 77.7 %copy-start.5 = (s32[8]{0:T(128)S(1)}, s32[8]{0:T(128)}, u32[]{:S(2)}) copy-start(s32[8]{0:T(128)} %param.13) | copy-start | bytes 100
  352.7 137.9 %all-reduce.5.cloned.1.call-start = ((), (), s32[]{:S(2)}) async-start(), calls=%async_computation.6 | async-start | bytes 393216 | tf_op jit(solution)/shard_map/psum | solution.py:54
  407.3 14.2 %slice-start = ((s8[6291456]{0:T(1024)(128)(4,1)}), s8[2097152]{0:T(1024)(128)(4,1)S(1)}, s32[]{:S(2)}) async-start(s8[6291456]{0:T(1024)(128)(4,1)} %bitcast.45), calls=%async_computation.7 | async-start | bytes 4194304
  411.3 10.1 %slice-start.1 = ((s8[6291456]{0:T(1024)(128)(4,1)}), s8[4194304]{0:T(1024)(128)(4,1)S(1)}, s32[]{:S(2)}) async-start(s8[6291456]{0:T(1024)(128)(4,1)} %bitcast.45), calls=%async_computation.8 | async-start | bytes 8388608
  425.6 323.6 %all-reduce.3.cloned.1.call-start = ((), (), s32[]{:S(2)}) async-start(), calls=%async_computation.5 | async-start | bytes 786432 | tf_op jit(solution)/shard_map/psum | solution.py:53
Sparse Core Ops, SparseCore 0:
  24.6 31.9 all-gather.1
  352.8 50.5 reduce-scatter.1
  425.7 64.7 all-reduce.4
  496.5 252.6 all-reduce.2
where the time goes:
time: 760 us; the launch traced here: 758 us
  waiting for transfers between devices  443 us (58%)
  blocking collectives  144 us (19%)
  local copies, waits for them, and re-layouts  87.5 us (12%)
  other arithmetic  43.3 us (6%)
  matrix products  16.6 us (2%)
  between operations  14 us (2%)
  starting transfers between devices  9.73 us (1%)
    psum x1, waiting for transfers between devices, per_device(): head_grad = lax.psum(head_part, ('tm', 'eval'))  257 us
    all_to_all x1, blocking collectives, per_device(): lax.all_to_all(group_grad, 'tm', split_axis=0, concat_axis=2, tiled=True)  83.4 us
    psum x1, blocking collectives, per_device(): totals = lax.psum(abs_sums, 'tm')  60.2 us
    psum x1, waiting for transfers between devices, per_device(): mod_grad = lax.psum(mod_part, 'eval')  53.9 us
    reduce_scatter x1, waiting for transfers between devices, per_device(): owner_grad = lax.psum_scatter(home, 'eval', scatter_dimension=2, tiled=True)  50.7 us
    all_to_all x1, waiting for transfers between devices, per_device(): lax.all_to_all(frame_whole, 'tm', split_axis=2, concat_axis=0, tiled=True)  48.5 us
    unnamed x20, local copies, waits for them, and re-layouts  38.7 us
    all_gather x1, waiting for transfers between devices, per_device(): frame_whole = lax.all_gather(latent, 'eval', axis=2, tiled=True)  32.2 us
  transfers between devices with their start and end apart: 5, of which 5 were waited for; matrix products, arithmetic and copies ran while one was open for 2% of the time, Pallas kernels for 0%

commit v1 on v0

--- a/solution.py
+++ b/solution.py
@@ -51,7 +51,8 @@
     head_part = jnp.einsum("fto,ftd->od", upstream, adapted, preferred_element_type=jnp.float32)
     mod_part = jnp.stack([jnp.sum(d_adapted, axis=1), jnp.sum(d_adapted * normed, axis=1)], axis=1)
     head_grad = lax.psum(head_part, ("tm", "eval"))
-    mod_grad = lax.psum(mod_part, "eval")
+    parts = lax.all_gather(mod_part, "eval", axis=0, tiled=False)
+    mod_grad = parts.sum(axis=0)
     d_normed = d_adapted * (1.0 + scale)
     d_hidden = inv_std * (
         d_normed

time: 760 us -> 716 us (0.942)
  waiting for transfers between devices: 443 us -> 399 us
    psum x1 -> x0, waiting for transfers between devices: 53.9 us -> none  [per_device(): mod_grad = lax.psum(mod_part, 'eval')]
    all_gather x0 -> x1, waiting for transfers between devices: none -> 12.9 us  [per_device(): parts = lax.all_gather(mod_part, 'eval', axis=0, tiled=False)]
    unnamed x20 -> x16, local copies, waits for them, and re-layouts: 38.7 us -> 37.8 us
  transfers between devices with their start and end apart: 5 -> 5, of which waited for: 5 -> 5; matrix products, arithmetic and copies ran while one was open for 2% -> 3% of each run, Pallas kernels for 0% -> 0%
where the time goes in v1:
time: 716 us; the launch traced here: 714 us
  waiting for transfers between devices  399 us (56%)
  blocking collectives  144 us (20%)
  local copies, waits for them, and re-layouts  84.1 us (12%)
  other arithmetic  44.9 us (6%)
  matrix products  18.6 us (3%)
  between operations  14 us (2%)
  starting transfers between devices  9.73 us (1%)
    psum x1, waiting for transfers between devices, per_device(): head_grad = lax.psum(head_part, ('tm', 'eval'))  255 us
    all_to_all x1, blocking collectives, per_device(): lax.all_to_all(group_grad, 'tm', split_axis=0, concat_axis=2, tiled=True)  83.4 us
    psum x1, blocking collectives, per_device(): totals = lax.psum(abs_sums, 'tm')  60.2 us
    reduce_scatter x1, waiting for transfers between devices, per_device(): owner_grad = lax.psum_scatter(home, 'eval', scatter_dimension=2, tiled=True)  50.7 us
    all_to_all x1, waiting for transfers between devices, per_device(): lax.all_to_all(frame_whole, 'tm', split_axis=2, concat_axis=0, tiled=True)  48.5 us
    unnamed x16, local copies, waits for them, and re-layouts  37.8 us
    all_gather x1, waiting for transfers between devices, per_device(): frame_whole = lax.all_gather(latent, 'eval', axis=2, tiled=True)  32.2 us
    scatter-add x1, other arithmetic, per_device(): group_grad = jnp.zeros(latent_all.shape, jnp.float32).at[frame_index.resh...  19.7 us
  transfers between devices with their start and end apart: 5, of which 5 were waited for; matrix products, arithmetic and copies ran while one was open for 3% of the time, Pallas kernels for 0%

profile of v1, /device:TPU:1, one launch (start us, length us, event | category | flops | bytes accessed | tf_op | source)
XLA Modules:
  0.0 714.2 jit_solution(7383057094747505891)
XLA Ops:
  7.2 3.8 convert_reduce_fusion
  11.1 4.6 fusion.13
  15.9 3.1 fusion.24
  19.0 3.2 copy.57
  22.2 2.3 copy.58
  24.5 32.2 %all-gather.4.cloned.1.call-done = bf16[16,16,4096]{2,1,0:T(8,128)(2,1)} async-done(((bf16[16,16,512]{2,1,0:T(8,128)(2,1)}), bf16[16,16,4096]{2,1,0:T(8,128)(2,1)}) %all-gather.4.cloned.1.call-update) | async-done | bytes 2097168 | tf_op jit(solution)/shard_map/all_gather | solution.py:29
  56.7 15.4 %copy.59 = bf16[16,16,4096]{1,0,2:T(8,128)(2,1)} copy(bf16[16,16,4096]{2,1,0:T(8,128)(2,1)} %all-gather.4.cloned.1.call-done) | data formatting | bytes 4194304 | tf_op jit(solution)/shard_map/all_gather | solution.py:29
  72.0 20.8 %reshape.133 = bf16[32,2,16384]{2,1,0:T(2,128)(2,1)} reshape(bf16[4096,16,16]{2,1,0:T(8,128)(2,1)} %bitcast.44) | data formatting | bytes 4194304
  92.8 9.6 %all-to-all-start = ((bf16[32,2,16384]{2,1,0:T(2,128)(2,1)}), bf16[32,2,16384]{2,1,0:T(2,128)(2,1)S(1)}, u32[]{:S(2)}, u32[]{:S(2)}) async-start(bf16[32,2,16384]{2,1,0:T(2,128)(2,1)} %reshape.133), calls=%async_computation | async-start | bytes 4194304 | tf_op jit(solution)/shard_map/all_to_all | solution.py:30
  102.8 48.5 %all-to-all-done = bf16[32,2,16384]{2,1,0:T(2,128)(2,1)S(1)} async-done(((bf16[32,2,16384]{2,1,0:T(2,128)(2,1)}), bf16[32,2,16384]{2,1,0:T(2,128)(2,1)S(1)}, u32[]{:S(2)}, u32[]{:S(2)}) %all-to-all-start) | async-done | bytes 2097184 | tf_op jit(solution)/shard_map/all_to_all | solution.py:30
  151.3 14.4 %reshape.134 = bf16[4096,16,16]{2,1,0:T(8,128)(2,1)} reshape(bf16[32,2,16384]{2,1,0:T(2,128)(2,1)S(1)} %all-to-all-done) | data formatting | bytes 4194304
  165.7 14.4 %copy.61 = bf16[32,16,16,128]{3,2,1,0:T(8,128)(2,1)S(1)} copy(bf16[32,16,16,128]{2,1,3,0:T(8,128)(2,1)} %bitcast.45) | data formatting | bytes 4194304 | tf_op jit(solution)/shard_map/all_to_all | solution.py:30
  183.1 60.2 %psum.14 = f32[8]{0:T(128)S(1)} all-reduce(f32[8]{0:T(128)S(1)} %fusion.22), channel_id=1, replica_groups=mesh['tm'=32,'eval'=8] {'tm'}, use_global_device_ids=true, to_apply=%region_3.0 | all-reduce | flops 8 | bytes 64 | tf_op jit(solution)/shard_map/psum | solution.py:37
  244.7 2.3 broadcast_in_dim.2
  247.0 19.7 %scatter_fusion = f32[512,16,128]{2,1,0:T(8,128)} fusion(f32[512,16,128]{2,1,0:T(8,128)} %broadcast_in_dim.2, s32[168]{0:T(256)S(1)} %bitcast.59, f32[168,16,128]{2,1,0:T(8,128)S(1)} %bitcast.50), kind=kCustom, calls=%fused_computation.1 | custom fusion | flops 344064 | bytes 4129440 | tf_op jit(solution)/shard_map/scatter-add | solution.py:44
  266.7 83.4 %all_to_all.36 = f32[512,16,128]{2,1,0:T(8,128)S(1)} all-to-all(f32[512,16,128]{2,1,0:T(8,128)} %scatter_fusion), channel_id=1, replica_groups=mesh['tm'=32,'eval'=8] {'tm'}, dimensions={0} | all-to-all | bytes 8388608 | tf_op jit(solution)/shard_map/all_to_all | solution.py:46
  350.1 2.5 copy.84
  352.7 50.7 %reduce-scatter.2.cloned.1.call-done = f32[16,16,512]{2,1,0:T(8,128)} async-done(((f32[16,16,4096]{2,1,0:T(8,128)}), f32[16,16,512]{2,1,0:T(8,128)}) %reduce-scatter.2.cloned.1.call-update) | async-done | bytes 524304 | tf_op jit(solution)/shard_map/reduce_scatter | solution.py:47
  406.5 2.4 copy.64
  408.8 10.0 %fusion.12 = (f32[16,1536]{1,0:T(8,128)S(1)}, f32[16,128]{1,0:T(8,128)S(1)}, f32[16,128]{1,0:T(8,128)S(1)}, f32[16,1536]{1,0:T(8,128)S(1)}, f32[16,128,1536]{2,1,0:T(8,128)}) fusion(bf16[16,128,1536]{2,1,0:T(8,128)(2,1)} %param.7, f32[16,128]{1,0:T(8,128)S(1)} %add_rsqrt_fusion, f32[16,128]{1,0:T(8,128)S(1)} %broadcast_multiply_fusion.2, ...), kind=kOutput, calls=%fused_computation.16 | convolution fusion | flops 434057216 | bytes 19660800 | tf_op jit(solution)/shard_map/fto,od->ftd/dot_general | solution.py:50
  419.6 5.6 fusion.18
  425.2 10.5 %fusion.11 = bf16[16,128,1536]{2,1,0:T(8,128)(2,1)} fusion(bf16[16,128,1536]{2,1,0:T(8,128)(2,1)} %param.7, f32[16,128,1536]{2,1,0:T(8,128)} %get-tuple-element.12, f32[16,128]{1,0:T(8,128)S(1)} %broadcast_multiply_fusion, f32[16,128]{1,0:T(8,128)S(1)} %broadcast_multiply_fusion.1, f32[16,1536]{1,0:T(8,128)S(1)} %get-tuple-element.14, ...), kind=kLoop, calls=%fused_computation.15 | loop fusion | flops 28311552 | bytes 25296896 | tf_op jit(solution)/shard_map/convert_element_type | solution.py:62
  435.7 12.9 %all-gather.6.cloned.1.call-done = f32[128,2,1536]{2,0,1:T(8,128)} async-done(((f32[16,2,1536]{2,0,1:T(8,128)}), f32[128,2,1536]{2,0,1:T(8,128)}) %all-gather.6.cloned.1.call-update) | async-done | bytes 1572880 | tf_op jit(solution)/shard_map/all_gather | solution.py:54
  451.0 255.0 %all-reduce.2.cloned.1.call-done = f32[64,1536]{1,0:T(8,128)} async-done(((f32[64,1536]{1,0:T(8,128)}), f32[64,1536]{1,0:T(8,128)}) %all-reduce.2.cloned.1.call-update) | async-done | bytes 393232 | tf_op jit(solution)/shard_map/psum | solution.py:53
  (42 shorter events, 12.9 us)
Async XLA Ops:
  7.2 8.7 %copy-start = (bf16[64,1536]{1,0:T(8,128)(2,1)S(1)}, bf16[64,1536]{1,0:T(8,128)(2,1)}, u32[]{:S(2)}) copy-start(bf16[64,1536]{1,0:T(8,128)(2,1)} %param.9) | copy-start | bytes 589828
  7.2 8.5 %copy-start.3 = (f32[16,2,1536]{2,1,0:T(2,128)S(1)}, f32[16,2,1536]{2,1,0:T(2,128)}, u32[]{:S(2)}) copy-start(f32[16,2,1536]{2,1,0:T(2,128)} %param.8) | copy-start | bytes 589828
  7.2 49.5 %all-gather.4.cloned.1.call-start = ((), (), s32[]{:S(2)}) async-start(), calls=%async_computation.3 | async-start | bytes 2359296 | tf_op jit(solution)/shard_map/all_gather | solution.py:29
  7.2 8.7 %copy-start.1 = (bf16[16,128,1536]{2,1,0:T(8,128)(2,1)S(1)}, bf16[16,128,1536]{2,1,0:T(8,128)(2,1)}, u32[]{:S(2)}) copy-start(bf16[16,128,1536]{2,1,0:T(8,128)(2,1)} %param.7) | copy-start | bytes 18874372
  72.0 30.4 %copy-start.4 = (s32[8]{0:T(128)S(1)}, s32[8]{0:T(128)}, u32[]{:S(2)}) copy-start(s32[8]{0:T(128)} %param.12) | copy-start | bytes 100
  92.8 58.5 %all-to-all-start = ((bf16[32,2,16384]{2,1,0:T(2,128)(2,1)}), bf16[32,2,16384]{2,1,0:T(2,128)(2,1)S(1)}, u32[]{:S(2)}, u32[]{:S(2)}) async-start(bf16[32,2,16384]{2,1,0:T(2,128)(2,1)} %reshape.133), calls=%async_computation | async-start | bytes 4194304 | tf_op jit(solution)/shard_map/all_to_all | solution.py:30
  102.4 301.0 %reduce-scatter.2.cloned.1.call-start = ((), (), s32[]{:S(2)}) async-start(), calls=%async_computation.4 | async-start | bytes 4718592 | tf_op jit(solution)/shard_map/reduce_scatter | solution.py:47
  165.7 16.0 %copy-start.2 = (bf16[8,21,16,128]{3,2,1,0:T(8,128)(2,1)S(1)}, bf16[8,21,16,128]{3,2,1,0:T(8,128)(2,1)}, u32[]{:S(2)}) copy-start(bf16[8,21,16,128]{3,2,1,0:T(8,128)(2,1)} %param.10) | copy-start | bytes 2064388
  165.7 77.7 %copy-start.5 = (s32[8]{0:T(128)S(1)}, s32[8]{0:T(128)}, u32[]{:S(2)}) copy-start(s32[8]{0:T(128)} %param.13) | copy-start | bytes 100
  352.7 95.9 %all-gather.6.cloned.1.call-start = ((), (), s32[]{:S(2)}) async-start(), calls=%async_computation.6 | async-start | bytes 1769472 | tf_op jit(solution)/shard_map/all_gather | solution.py:54
  419.5 286.4 %all-reduce.2.cloned.1.call-start = ((), (), s32[]{:S(2)}) async-start(), calls=%async_computation.5 | async-start | bytes 786432 | tf_op jit(solution)/shard_map/psum | solution.py:53
Sparse Core Ops, SparseCore 0:
  24.6 31.9 all-gather.3
  352.8 50.5 reduce-scatter.1
  419.6 28.9 all-gather.5
  454.6 251.3 all-reduce.1
